TPU v7x, 256 devices: a whole 4x4x8 slice. The times are simulated.
256 devices in a mesh: req: 64 (over y, x_lo, z), tp: 4 (over x_hi, core).
Axes of the slice: x: 4 (x_hi: 2, x_lo: 2; x = x_hi * 2 + x_lo), y: 4, z: 8, core: 2. Of those that a mesh axis runs over, the one named last changes fastest.
Arguments:
- queries: bfloat16 [65536, 2560], P('req', 'tp'), may hold values from -51 to 51
- fresh_keys: bfloat16 [65536, 2560], P('req', 'tp'), may hold values from -5 to 5
- fresh_values: bfloat16 [65536, 2560], P('req', 'tp'), may hold values from -24 to 24
- paged_keys: bfloat16 [1024, 128, 2560], P('req', None, 'tp'), may hold values from -6 to 6
- paged_values: bfloat16 [1024, 128, 2560], P('req', None, 'tp'), may hold values from -24 to 24
- request_page_table: int32 [512, 8], P('req'), may hold values from 0 to 15, as said below
- live_token_count: int32 [512], P('req'), may hold values from 2 to 128, as said below
- request_adapter_slot: int32 [512], P('req'), may hold values from 0 to 15
- adapters_in_use: int32 [16], replicated, may hold values from 0 to 63, as said below
- adapter_pool_row: int32 [64], replicated, may hold values from 0 to 63, each once
- adapter_down_factors: bfloat16 [64, 16, 2560], P('req', None, 'tp'), may hold values from -0.125 to 0.125
- adapter_up_factors: bfloat16 [64, 16, 2560], P('req'), may hold values from -1.5 to 1.5
- output_weight: bfloat16 [2560, 2560], P('tp'), may hold values from -0.125 to 0.125
- gating: float32 [512, 2560], P('req'), may hold values from 1 to 4
Outputs:
- gated: bfloat16 [65536, 2560], P(('req', 'tp'))
Inputs may be any that keep to these rules, and one draw needn't show every extreme that they name: `request_page_table`: A request's 8 pages are distinct. `live_token_count`: some request has all 128 slots live. `adapters_in_use`: 16 distinct adapter ids.
All inputs are finite; a program needn't handle non-finite values.
Results may differ from a plain program's by a relative error of at most 0.0057.
Values may be sent and summed in bfloat16 or wider, within the bound.
A program may use at most 192 MiB of HBM per device.

v0:
```python
import math

import jax
import jax.numpy as jnp
from jax import lax
from jax.sharding import PartitionSpec as P

HD = 128
ADAPTER_RANK = 16


def sent_together(arrays, axis, dim, along):
    both = jnp.concatenate(arrays, axis=along)
    result, at, done = (lax.all_gather(both, axis, axis=dim, tiled=True), 0, [])
    for a in arrays:
        done.append(lax.slice_in_dim(result, at, at + a.shape[along], axis=along))
        at += a.shape[along]
    return tuple(done)


def from_everyone(x, axis):
    copies = jnp.broadcast_to(x, (lax.axis_size(axis), *x.shape))
    return lax.all_to_all(copies, axis, split_axis=0, concat_axis=0, tiled=True)


def taken_together(x, axis):
    everything = from_everyone(x, axis)
    return jnp.sum(everything, axis=0)


def attend(
    queries,
    fresh_keys,
    fresh_values,
    paged_keys,
    paged_values,
    request_page_table,
    live_token_count,
):
    requests_here = live_token_count.shape[0]
    slot_count = queries.shape[0] // requests_here
    feature_width = queries.shape[1]
    heads_here = feature_width // HD
    cached_keys = paged_keys[request_page_table].reshape(requests_here, -1, feature_width)
    cached_values = paged_values[request_page_table].reshape(requests_here, -1, feature_width)
    cached = cached_keys.shape[1]
    keys_all = jnp.concatenate(
        [cached_keys, fresh_keys.reshape(requests_here, slot_count, feature_width)], axis=1
    )
    keys_all = keys_all.reshape(requests_here, -1, heads_here, HD)
    values_all = jnp.concatenate(
        [cached_values, fresh_values.reshape(requests_here, slot_count, feature_width)], axis=1
    )
    values_all = values_all.reshape(requests_here, -1, heads_here, HD)
    query_heads = queries.reshape(requests_here, slot_count, heads_here, HD)
    scores = jnp.einsum(
        "rqhd,rkhd->rhqk", query_heads, keys_all, preferred_element_type=jnp.float32
    ) * (1.0 / math.sqrt(HD))
    key_index = jnp.arange(keys_all.shape[1])
    usable = (key_index[None, :] < cached) | (
        key_index[None, :] - cached < live_token_count[:, None]
    )
    scores = jnp.where(usable[:, None, None, :], scores, -1e30)
    row_peak = jnp.max(scores, axis=-1, keepdims=True)
    weights = jnp.exp(scores - row_peak)
    row_total = jnp.sum(weights, axis=-1)
    rounded = weights.astype(jnp.bfloat16)
    blended = jnp.einsum("rhqk,rkhd->rqhd", rounded, values_all, preferred_element_type=jnp.float32)
    blended = blended / jnp.swapaxes(row_total, 1, 2)[..., None]
    live_slots = jnp.arange(slot_count)[None, :] < live_token_count[:, None]
    blended = jnp.where(live_slots[:, :, None, None], blended, 0.0)
    return blended.reshape(requests_here * slot_count, feature_width).astype(jnp.bfloat16)


def body(
    queries,
    fresh_keys,
    fresh_values,
    paged_keys,
    paged_values,
    request_page_table,
    live_token_count,
    request_adapter_slot,
    adapters_in_use,
    adapter_pool_row,
    adapter_down_factors,
    adapter_up_factors,
    output_weight,
    gating,
):
    attention_output = attend(
        queries,
        fresh_keys,
        fresh_values,
        paged_keys,
        paged_values,
        request_page_table,
        live_token_count,
    )
    requests_here = live_token_count.shape[0]
    tok_rows = attention_output.shape[0]
    slot_count = tok_rows // requests_here
    feature_width = attention_output.shape[1]
    output_width = adapter_up_factors.shape[2]
    holder_active = adapter_pool_row[adapters_in_use]
    active_count = adapters_in_use.shape[0]
    pieces = sent_together((adapter_down_factors, adapter_up_factors), "req", 0, 2)
    length = pieces[0].shape[0]
    select = (holder_active[:, None] == jnp.arange(length)[None, :]).astype(jnp.bfloat16)
    down_add = jnp.einsum("an,nkh->akh", select, pieces[0], preferred_element_type=jnp.float32)
    up_add = jnp.einsum("an,nkh->akh", select, pieces[1], preferred_element_type=jnp.float32)
    down_active = down_add.astype(jnp.bfloat16)
    up_active = up_add.astype(jnp.bfloat16)
    chooser = (request_adapter_slot[:, None] == jnp.arange(active_count)[None, :]).astype(
        jnp.bfloat16
    )
    down_table = jnp.einsum(
        "ra,akh->rkh", chooser, down_active, preferred_element_type=jnp.float32
    ).astype(jnp.bfloat16)
    down_table = down_table.reshape(requests_here * ADAPTER_RANK, feature_width)
    up_factor_table = jnp.einsum(
        "ra,akn->rkn", chooser, up_active, preferred_element_type=jnp.float32
    ).reshape(requests_here * ADAPTER_RANK, output_width)
    rank_all = lax.dot_general(
        attention_output, down_table, (((1,), (1,)), ((), ())), preferred_element_type=jnp.float32
    )
    row_owner = jnp.arange(tok_rows) // slot_count
    col_owner = jnp.arange(requests_here * ADAPTER_RANK) // ADAPTER_RANK
    rank_activations = jnp.where(row_owner[:, None] == col_owner[None, :], rank_all, 0.0)
    own_rows = tok_rows // lax.axis_size("tp")
    row_start = lax.axis_index("tp") * own_rows
    adapter_update = lax.psum_scatter(
        jnp.dot(attention_output, output_weight, preferred_element_type=jnp.float32),
        "tp",
        scatter_dimension=0,
        tiled=True,
    )
    rank_sum = taken_together(rank_activations, "tp")
    rank_own = lax.dynamic_slice_in_dim(rank_sum, row_start, own_rows, 0)
    adapter_update = adapter_update + jnp.dot(
        rank_own, up_factor_table, precision=lax.Precision.HIGHEST
    )
    slot_owner = (row_start + jnp.arange(own_rows)) // slot_count
    gate_select = (slot_owner[:, None] == jnp.arange(requests_here)[None, :]).astype(jnp.float32)
    gate_rows = jnp.dot(gate_select, gating, precision=lax.Precision.HIGHEST)
    return (gate_rows * adapter_update).astype(jnp.bfloat16)


def solution(mesh):
    return jax.shard_map(
        body,
        mesh=mesh,
        in_specs=(
            P("req", "tp"),
            P("req", "tp"),
            P("req", "tp"),
            P("req", None, "tp"),
            P("req", None, "tp"),
            P("req", None),
            P("req"),
            P("req"),
            P(),
            P(),
            P("req", None, "tp"),
            P("req", None, None),
            P("tp", None),
            P("req", None),
        ),
        out_specs=P(("req", "tp"), None),
        check_vma=False,
    )
```

profile of v0, /device:TPU:1, one launch (start us, length us, event | category | flops | bytes accessed | tf_op | source)
XLA Modules:
  0.0 378.6 jit_solution(814878003398017056)
XLA Ops:
  9.9 8.5 %gather_fusion.1 = bf16[64,128,640]{2,1,0:T(8,128)(2,1)} fusion(bf16[16,128,640]{2,1,0:T(8,128)(2,1)} %param.17, s32[1024]{0:T(1024)S(1)} %pad_clamp_fusion.1), kind=kCustom, calls=%fused_computation.1 | custom fusion | bytes 20971776 | tf_op jit(solution)/shard_map/gather | solution.py:44
  18.4 23.6 %reshape.177 = bf16[8,1024,5,128]{3,2,1,0:T(8,128)(2,1)} reshape(bf16[64,128,640]{2,1,0:T(8,128)(2,1)} %gather_fusion.1) | data formatting | bytes 20971520 | tf_op jit(solution)/shard_map/concatenate | solution.py:47
  42.0 12.4 %copy.53 = bf16[8,1024,5,128]{3,1,2,0:T(8,128)(2,1)} copy(bf16[8,1024,5,128]{3,2,1,0:T(8,128)(2,1)} %reshape.177) | data formatting | bytes 20971520 | tf_op jit(solution)/shard_map/concatenate | solution.py:47
  54.4 4.1 %reshape.178 = bf16[8,128,5,128]{3,2,1,0:T(8,128)(2,1)} reshape(bf16[1024,640]{1,0:T(8,128)(2,1)} %param.15) | data formatting | bytes 2621440 | tf_op jit(solution)/shard_map/concatenate | solution.py:47
  58.5 3.0 copy.54
  61.5 4.1 %reshape.179 = bf16[8,128,5,128]{3,2,1,0:T(8,128)(2,1)} reshape(bf16[1024,640]{1,0:T(8,128)(2,1)} %param.14) | data formatting | bytes 2621440 | tf_op jit(solution)/shard_map/reshape | solution.py:55
  65.6 8.5 %gather_fusion = bf16[64,128,640]{2,1,0:T(8,128)(2,1)} fusion(bf16[16,128,640]{2,1,0:T(8,128)(2,1)} %param.18, s32[1024]{0:T(1024)S(1)} %pad_clamp_fusion.1), kind=kCustom, calls=%fused_computation | custom fusion | bytes 20971776 | tf_op jit(solution)/shard_map/gather | solution.py:45
  74.0 23.6 %reshape.175 = bf16[8,1024,5,128]{3,2,1,0:T(8,128)(2,1)} reshape(bf16[64,128,640]{2,1,0:T(8,128)(2,1)} %gather_fusion) | data formatting | bytes 20971520 | tf_op jit(solution)/shard_map/concatenate | solution.py:51
  97.7 20.9 %copy.49 = bf16[8,1024,5,128]{1,3,2,0:T(8,128)(2,1)} copy(bf16[8,1024,5,128]{3,2,1,0:T(8,128)(2,1)} %reshape.175) | data formatting | bytes 20971520 | tf_op jit(solution)/shard_map/concatenate | solution.py:51
  118.6 4.1 %reshape.176 = bf16[8,128,5,128]{3,2,1,0:T(8,128)(2,1)} reshape(bf16[1024,640]{1,0:T(8,128)(2,1)} %param.16) | data formatting | bytes 2621440 | tf_op jit(solution)/shard_map/concatenate | solution.py:51
  122.7 3.7 copy.50
  126.6 16.2 %bitcast_reduce_fusion = (f32[8,5,128]{2,1,0:T(8,128)S(1)}, f32[8,5,1152,128]{3,2,1,0:T(8,128)}) fusion(pred[8,1152]{1,0:T(8,128)(4,1)S(1)} %compare_or_fusion, bf16[8,128,5,128]{3,2,1,0:T(8,128)(2,1)} %reshape.179, bf16[8,128,5,128]{3,1,2,0:T(8,128)(2,1)} %copy.54, bf16[8,1024,5,128]{3,1,2,0:T(8,128)(2,1)} %copy.53), kind=kOutput, calls=%fused_computation.4 | convolution fusion | flops 1551232000 | bytes 36729856 | tf_op jit(solution)/shard_map/rqhd,rkhd->rhqk/dot_general | solution.py:56
  142.8 11.0 %fusion.1 = f32[8,5,128]{2,1,0:T(8,128)S(1)} fusion(f32[8,5,1152,128]{3,2,1,0:T(8,128)} %get-tuple-element.6, f32[8,5,128]{2,1,0:T(8,128)S(1)} %get-tuple-element.5, pred[8,1152]{1,0:T(8,128)(4,1)S(1)} %compare_or_fusion), kind=kLoop, calls=%fused_computation.7 | loop fusion | flops 23587840 | bytes 23643136 | tf_op jit(solution)/shard_map/reduce_sum | solution.py:66
  153.7 16.4 %fusion.24 = bf16[8,128,5,128]{1,3,2,0:T(8,128)(2,1)} fusion(f32[8,5,1152,128]{3,2,1,0:T(8,128)} %get-tuple-element.6, f32[8,5,128]{2,1,0:T(8,128)S(1)} %get-tuple-element.5, pred[8,1152]{1,0:T(8,128)(4,1)S(1)} %compare_or_fusion, bf16[8,128,5,128]{1,3,2,0:T(8,128)(2,1)} %copy.50, bf16[8,1024,5,128]{1,3,2,0:T(8,128)(2,1)} %copy.49, ...), kind=kOutput, calls=%fused_computation.29 | convolution fusion | flops 1559101440 | bytes 36751360 | tf_op jit(solution)/shard_map/rhqk,rkhd->rqhd/dot_general | solution.py:68
  173.4 6.8 %fusion.34 = f32[1024,2560]{1,0:T(8,128)} fusion(bf16[640,2560]{1,0:T(8,128)(2,1)S(1)} %copy-done, bf16[80,8,8,128]{3,2,1,0:T(8,128)(2,1)S(1)} %bitcast.46), kind=kOutput, calls=%fused_computation.33 | convolution fusion | flops 3355443200 | bytes 15073280 | tf_op jit(solution)/shard_map/dot_general | solution.py:133
  181.6 101.6 %all-gather.2.cloned.1.call-done = bf16[64,16,3200]{2,1,0:T(8,128)(2,1)} async-done(((bf16[1,16,3200]{2,1,0:T(8,128)(2,1)}), bf16[64,16,3200]{2,1,0:T(8,128)(2,1)}) %all-gather.2.cloned.1.call-update) | async-done | bytes 6553616 | tf_op jit(solution)/shard_map/all_gather | solution.py:14
  290.9 44.8 %all-to-all-start = ((f32[4,1024,128]{2,1,0:T(8,128)}), f32[4,1024,128]{2,1,0:T(8,128)}, u32[]{:S(2)}, u32[]{:S(2)}) async-start(f32[4,1024,128]{2,1,0:T(8,128)} %broadcast_in_dim.62), calls=%async_computation.1 | async-start | bytes 4194304 | tf_op jit(solution)/shard_map/all_to_all | solution.py:23
  335.8 2.7 fusion.54
  338.5 5.2 %slice.15 = bf16[64,16,2560]{2,1,0:T(8,128)(2,1)} slice(bf16[64,16,3200]{2,1,0:T(8,128)(2,1)} %all-gather.2.cloned.1.call-done), slice={[0:64], [0:16], [640:3200]} | slice | bytes 10485760 | tf_op jit(solution)/shard_map/slice | solution.py:16
  343.7 9.4 %fusion.30 = f32[8,16,2560]{2,0,1:T(8,128)} fusion(bf16[64,16,2560]{2,1,0:T(8,128)(2,1)} %slice.15, s32[16]{0:T(128)S(1)} %gather_fusion.2, s32[8]{0:T(128)S(1)} %copy-done.4), kind=kOutput, calls=%fused_computation.30 | convolution fusion | flops 95028352 | bytes 6553696 | tf_op jit(solution)/shard_map/ra,akn->rkn/dot_general | solution.py:121
  353.0 3.1 copy.62
  356.2 6.0 %all-to-all-done = f32[4,1024,128]{2,1,0:T(8,128)} async-done(((f32[4,1024,128]{2,1,0:T(8,128)}), f32[4,1024,128]{2,1,0:T(8,128)}, u32[]{:S(2)}, u32[]{:S(2)}) %all-to-all-start) | async-done | bytes 2097184 | tf_op jit(solution)/shard_map/all_to_all | solution.py:23
  362.2 2.5 reduce_sum.19
  364.8 6.4 %fusion.19 = bf16[256,2560]{1,0:T(8,128)(2,1)} fusion(f32[256,2560]{1,0:T(8,128)} %fusion.54, f32[256,2560]{1,0:T(8,128)} %reduce-scatter.2.cloned.1.call-done, f32[128,2560]{1,0:T(8,128)} %bitcast.48, f32[1024,128]{1,0:T(8,128)} %reduce_sum.19, s32[]{:T(128)S(6)} %select_n.61), kind=kOutput, calls=%fused_computation.25 | convolution fusion | flops 1008599040 | bytes 7995396 | tf_op jit(solution)/shard_map/dot_general | solution.py:140
  (39 shorter events, 15.0 us)
Async XLA Ops:
  7.4 166.0 %copy-start = (bf16[640,2560]{1,0:T(8,128)(2,1)S(1)}, bf16[640,2560]{1,0:T(8,128)(2,1)}, u32[]{:S(2)}) copy-start(bf16[640,2560]{1,0:T(8,128)(2,1)} %param.26) | copy-start | bytes 9830404
  7.4 275.8 %all-gather.2.cloned.1.call-start = ((), (), s32[]{:S(2)}) async-start(), calls=%async_computation.3 | async-start | bytes 6656000 | tf_op jit(solution)/shard_map/all_gather | solution.py:14
  9.1 355.7 %reduce-scatter.2.cloned.1.call-start = ((), (), s32[]{:S(2)}) async-start(), calls=%async_computation.2 | async-start | bytes 13107200 | tf_op jit(solution)/shard_map/reduce_scatter | solution.py:132
  118.6 7.8 %copy-start.5 = (s32[8]{0:T(128)S(1)}, s32[8]{0:T(128)}, u32[]{:S(2)}) copy-start(s32[8]{0:T(128)} %param.20) | copy-start | bytes 100
  172.3 1.1 copy-start.2
  180.2 0.7 copy-start.6
  180.2 0.7 copy-start.1
  180.2 105.5 %copy-start.4 = (s32[8]{0:T(128)S(1)}, s32[8]{0:T(128)}, u32[]{:S(2)}) copy-start(s32[8]{0:T(128)} %param.21) | copy-start | bytes 100
  285.7 50.1 %copy-start.3 = (f32[8,2560]{1,0:T(8,128)S(1)}, f32[8,2560]{1,0:T(8,128)}, u32[]{:S(2)}) copy-start(f32[8,2560]{1,0:T(8,128)} %param.27) | copy-start | bytes 245764
  290.9 71.3 %all-to-all-start = ((f32[4,1024,128]{2,1,0:T(8,128)}), f32[4,1024,128]{2,1,0:T(8,128)}, u32[]{:S(2)}, u32[]{:S(2)}) async-start(f32[4,1024,128]{2,1,0:T(8,128)} %broadcast_in_dim.62), calls=%async_computation.1 | async-start | bytes 4194304 | tf_op jit(solution)/shard_map/all_to_all | solution.py:23
Sparse Core Ops, SparseCore 0:
  10.0 273.1 all-gather.1
Sparse Core Ops, SparseCore 1:
  180.3 115.9 reduce-scatter.1
where the time goes:
time: 381 us; the launch traced here: 379 us
  local copies, waits for them, and re-layouts  133 us (35%)
  waiting for transfers between devices  108 us (28%)
  matrix products  61.6 us (16%)
  starting transfers between devices  44.9 us (12%)
  other arithmetic  16.1 us (4%)
  between operations  14.9 us (4%)
    all_gather x1, waiting for transfers between devices, sent_together(): result, at, done = (lax.all_gather(both, axis, axis=dim, tiled=True), 0, [])  102 us
    concatenate x4, local copies, waits for them, and re-layouts, attend(): jnp.concatenate([cached_values, fresh_values.reshape(requests_here, slot_...  52.4 us
    all_to_all x1, starting transfers between devices, from_everyone(): return lax.all_to_all(copies, axis, split_axis=0, concat_axis=0, tiled=True)  44.8 us
    concatenate x4, local copies, waits for them, and re-layouts, attend(): jnp.concatenate([cached_keys, fresh_keys.reshape(requests_here, slot_coun...  43.1 us
    dot_general x1, matrix products, attend(): jnp.einsum('rhqk,rkhd->rqhd', rounded, values_all, preferred_element_type...  16.4 us
    dot_general x1, matrix products, attend(): jnp.einsum('rqhd,rkhd->rhqk', query_heads, keys_all, preferred_element_ty...  16.2 us
    reduce_sum x1, other arithmetic, attend(): row_total = jnp.sum(weights, axis=-1)  11 us
    dot_general x1, matrix products, body(): jnp.einsum('ra,akn->rkn', chooser, up_active, preferred_element_type=jnp....  9.35 us
  transfers between devices with their start and end apart: 3, of which 2 were waited for; matrix products, arithmetic and copies ran while one was open for 53% of the time, Pallas kernels for 0%

commit v1 on v0

v1 whole, which is shorter than its diff:
```python
import functools
import math

import jax
import jax.numpy as jnp
from jax import lax
from jax.experimental import pallas as pl
from jax.experimental.pallas import tpu as pltpu
from jax.sharding import PartitionSpec as P

HD = 128
RANK = 16
MESH = pl.DeviceIdType.MESH
NEG = -1e30
SCALE = math.log2(math.e) / math.sqrt(HD)
BF = jnp.bfloat16
F32 = jnp.float32
Y, XLO, Z = 4, 2, 8


def kernel(
    q_hbm, fk_hbm, fv_hbm, kp_hbm, vp_hbm, down_hbm, up_hbm, w_hbm, gate_hbm,
    pt, live, slot_of, in_use, pool_row,
    out_hbm,
    q, fk, fv, kp, vp, w, gate,
    att, psend, precv, pkeep, xsend, csend, crecv, acc, xrecv, stage,
    zbuf, ybuf, xbuf, slots, rbuf, ubuf, rsend, usend,
    lsem, osem,
    p_s, p_r, x_s, x_r, c_s, c_r, z_s, z_r, y_s, y_r, xl_s, xl_r, s_s, s_r, ra_s, ra_r, u_s, u_r,
):
    req = lax.axis_index("req")
    tp = lax.axis_index("tp")
    z = lax.rem(req, Z)
    yx = req // Z
    y = yx // XLO
    xlo = lax.rem(yx, XLO)
    hi = tp // 2
    core = lax.rem(tp, 2)
    width = q.shape[1]
    heads = width // HD
    n_out = w.shape[1]
    half = n_out // 2

    def at(y_, xlo_, z_):
        return (y_ * XLO + xlo_) * Z + z_

    partner = (req, hi * 2 + 1 - core)
    tp_peer = lambda d: (req, lax.rem(tp + d, 4))
    z_peer = lambda d: (at(y, xlo, lax.rem(z + d, Z)), tp)
    y_peer = lambda d: (at(lax.rem(y + d, Y), xlo, z), tp)
    xlo_peer = (at(y, 1 - xlo, z), tp)

    first = pl.multiple_of((1 - hi) * 512, 512)
    second = pl.multiple_of(hi * 512, 512)
    loads = []

    def load(src, dst):
        cp = pltpu.make_async_copy(src, dst, lsem.at[len(loads)])
        cp.start()
        loads.append(cp)
        return cp

    own_down = load(down_hbm.at[0], zbuf.at[0, pl.ds(0, RANK)])
    own_up = load(up_hbm.at[0, :, pl.ds(pl.multiple_of(tp * width, width), width)], zbuf.at[0, pl.ds(RANK, RANK)])
    early = [
        load(kp_hbm, kp),
        load(q_hbm.at[pl.ds(first, 512)], q.at[pl.ds(first, 512)]),
        load(fk_hbm.at[pl.ds(first, 512)], fk.at[pl.ds(first, 512)]),
        load(vp_hbm, vp),
        load(fv_hbm.at[pl.ds(first, 512)], fv.at[pl.ds(first, 512)]),
    ]
    load_w = load(w_hbm, w)
    late = [
        load(q_hbm.at[pl.ds(second, 512)], q.at[pl.ds(second, 512)]),
        load(fk_hbm.at[pl.ds(second, 512)], fk.at[pl.ds(second, 512)]),
        load(fv_hbm.at[pl.ds(second, 512)], fv.at[pl.ds(second, 512)]),
        load(gate_hbm, gate),
    ]

    barrier = pltpu.get_barrier_semaphore()
    peers = [tp_peer(d) for d in range(1, 4)] + [z_peer(d) for d in range(1, Z)]
    peers += [y_peer(d) for d in range(1, Y)] + [xlo_peer]
    for p in peers:
        pl.semaphore_signal(barrier, inc=1, device_id=p, device_id_type=MESH)
    pl.semaphore_wait(barrier, len(peers))

    def remote(src, dst, ss, rs, dev):
        return pltpu.make_async_remote_copy(src, dst, ss, rs, device_id=dev, device_id_type=MESH)

    z_copy = lambda d: remote(zbuf.at[0], zbuf.at[d], z_s.at[d], z_r.at[d], z_peer(d))
    y_copy = lambda d: remote(ybuf.at[0], ybuf.at[d], y_s.at[d], y_r.at[d], y_peer(d))
    xl_copy = lambda: remote(xbuf.at[0], xbuf.at[1], xl_s.at[0], xl_r.at[0], xlo_peer)
    s_copy = lambda d: remote(slots.at[0], slots.at[d], s_s.at[d], s_r.at[d], z_peer(d))

    own_down.wait()
    own_up.wait()
    for d in range(1, Z):
        z_copy(d).start()

    def phase_y():
        for d in range(1, Z):
            z_copy(d).wait_recv()
        for k in range(2):
            holder = pool_row[in_use[2 * z + k]]
            row = zbuf[lax.rem(z - lax.rem(holder, Z) + Z, Z)]
            ybuf[0, k] = jnp.where(holder // Z == yx, row.astype(F32), 0.0).astype(BF)
        for d in range(1, Y):
            y_copy(d).start()

    def phase_x():
        for d in range(1, Y):
            y_copy(d).wait_recv()
        total = ybuf[0].astype(F32) + ybuf[1].astype(F32) + ybuf[2].astype(F32) + ybuf[3].astype(F32)
        xbuf[0] = total.astype(BF)
        xl_copy().start()

    def phase_z():
        xl_copy().wait_recv()
        slots[0] = (xbuf[0].astype(F32) + xbuf[1].astype(F32)).astype(BF)
        for d in range(1, Z):
            s_copy(d).start()

    p_copy = lambda j: remote(psend.at[j], precv.at[j], p_s.at[j], p_r.at[j], partner)
    c_copy = lambda k: remote(csend.at[k], crecv.at[k], c_s.at[k], c_r.at[k], partner)

    def x_copy(j):
        return remote(
            xsend.at[j], xrecv.at[lax.rem(j, 2), core],
            x_s.at[j], x_r.at[lax.rem(j, 2), core],
            (req, (1 - hi) * 2 + j // 2),
        )

    def project(a, base, chunk):
        return jnp.dot(
            a, w[:, pl.ds(pl.multiple_of(base, 128), chunk)], preferred_element_type=F32
        )

    mine = pl.multiple_of(core * half, half)
    other = pl.multiple_of((1 - core) * half, half)
    CH = 640

    def pickup(j):
        p_copy(j).wait_recv()
        for n in range(0, half, CH):
            cols = pl.ds(n, CH)
            xsend[j, :, cols] = (pkeep[j, :, cols] + precv[j, :, cols].astype(F32)).astype(BF)
        x_copy(j).start()

    def request_of(step):
        there = (1 - hi) * 4 + step
        partners = hi * 4 + (1 - core) * 2 + step - 4
        own = hi * 4 + core * 2 + step - 6
        return jnp.where(step < 4, there, jnp.where(step < 6, partners, own))

    def head(r, h, pages, count):
        cols = pl.ds(h * HD, HD)
        rows = pl.ds(pl.multiple_of(r * 128, 128), 128)
        qh = q[rows, cols]
        contract = (((1,), (1,)), ((), ()))
        parts = []
        for g in range(0, 8, 2):
            k2 = jnp.concatenate([kp[pages[g], :, cols], kp[pages[g + 1], :, cols]], axis=0)
            parts.append(lax.dot_general(qh, k2, contract, preferred_element_type=F32))
        fresh = lax.dot_general(qh, fk[rows, cols], contract, preferred_element_type=F32)
        key_at = lax.broadcasted_iota(jnp.int32, fresh.shape, 1)
        parts.append(jnp.where(key_at < count, fresh, NEG))
        s = jnp.concatenate(parts, axis=1)
        peak = jnp.max(s, axis=1, keepdims=True)
        p = jnp.exp2((s - peak) * SCALE)
        total = jnp.sum(p, axis=1, keepdims=True)
        v = jnp.concatenate([vp[pages[g], :, cols] for g in range(8)] + [fv[rows, cols]], axis=0)
        o = jnp.dot(p.astype(BF), v, preferred_element_type=F32)
        o = o / total
        slot_at = lax.broadcasted_iota(jnp.int32, o.shape, 0)
        att[r, :, cols] = jnp.where(slot_at < count, o, 0.0).astype(BF)

    for cp in early:
        cp.wait()

    def step_body(step, carry):
        r = request_of(step)
        pages = [pt[r, g] for g in range(8)]
        count = live[r]

        @pl.when(step == 4)
        def _():
            for cp in late:
                cp.wait()

        for h in range(2):
            head(r, h, pages, count)

        @pl.when((step >= 1) & (step <= 4))
        def _():
            pickup(step - 1)

        for h in range(2, heads):
            head(r, h, pages, count)

        @pl.when(step == 0)
        def _():
            load_w.wait()

        a = att[r]

        @pl.when(step < 4)
        def _():
            for n in range(0, half, CH):
                psend[step, :, pl.ds(n, CH)] = project(a, other + n, CH).astype(BF)
            p_copy(step).start()
            for n in range(0, half, CH):
                pkeep[step, :, pl.ds(n, CH)] = project(a, mine + n, CH)

        @pl.when((step >= 4) & (step < 6))
        def _():
            for n in range(0, n_out, CH):
                csend[step - 4, :, pl.ds(n, CH)] = project(a, n, CH).astype(BF)
            c_copy(step - 4).start()

        @pl.when(step >= 6)
        def _():
            for n in range(0, n_out, CH):
                acc[step - 6, :, pl.ds(n, CH)] = project(a, n, CH)

        @pl.when(step == 0)
        def _():
            phase_y()

        @pl.when(step == 2)
        def _():
            phase_x()

        @pl.when(step == 3)
        def _():
            phase_z()

        return carry

    lax.fori_loop(0, 8, step_body, 0)

    for d in range(1, Z):
        s_copy(d).wait_recv()
    ra_copy = lambda d: remote(rsend.at[d], rbuf.at[d], ra_s.at[d], ra_r.at[d], tp_peer(d))
    u_copy = lambda d: remote(usend.at[d], ubuf.at[d], u_s.at[d], u_r.at[d], tp_peer(d))
    for d in (2, 3, 1, 0):
        for k in range(2):
            r = lax.rem(tp + d, 4) * 2 + k
            s = slot_of[r]
            place = lax.rem(z - s // 2 + Z, Z)
            factors = slots[place, lax.rem(s, 2)]
            ranked = lax.dot_general(
                factors[:RANK], att[r], (((1,), (1,)), ((), ())), preferred_element_type=F32
            )
            if d == 0:
                rbuf[0, k] = ranked
                ubuf[0, k] = factors[RANK:]
            else:
                rsend[d, k] = ranked
                usend[d, k] = factors[RANK:]
        if d:
            ra_copy(d).start()
            u_copy(d).start()

    for k in range(2):
        c_copy(k).wait_recv()
    for d in range(1, 4):
        ra_copy(d).wait_recv()
        u_copy(d).wait_recv()

    for k in range(2):
        ra = rbuf[0, k] + rbuf[1, k] + rbuf[2, k] + rbuf[3, k]
        top = ra.astype(BF)
        rest = ra - top.astype(F32)
        mid = rest.astype(BF)
        low = (rest - mid.astype(F32)).astype(BF)
        ra3 = jnp.concatenate([top, mid, low], axis=0)
        for n in range(4):
            cols = pl.ds(n * width, width)
            u1 = ubuf[lax.rem(tp - n + 4, 4), k]
            u3 = jnp.concatenate([u1, u1, u1], axis=0)
            term = lax.dot_general(ra3, u3, (((0,), (0,)), ((), ())), preferred_element_type=F32)
            acc[k, :, cols] = acc[k, :, cols] + crecv[k, :, cols].astype(F32) + term

    outs = []
    for k in range(2):
        g_row = tp * 2 + k
        for cs in range(2):
            remote(xsend.at[0], xrecv.at[k, cs], x_s.at[0], x_r.at[k, cs], partner).wait_recv()
            for n in range(0, half, CH):
                cols = pl.ds(cs * half + n, CH)
                total = acc[k, :, cols] + xrecv[k, cs, :, pl.ds(n, CH)].astype(F32)
                stage[k, :, cols] = (gate[pl.ds(g_row, 1), cols] * total).astype(BF)
            block = (pl.ds(k * 128, 128), pl.ds(cs * half, half))
            cp = pltpu.make_async_copy(
                stage.at[k, :, pl.ds(cs * half, half)], out_hbm.at[block], osem.at[k, cs]
            )
            cp.start()
            outs.append(cp)

    for d in range(1, Z):
        z_copy(d).wait_send()
        s_copy(d).wait_send()
    for d in range(1, Y):
        y_copy(d).wait_send()
    xl_copy().wait_send()
    for j in range(4):
        p_copy(j).wait_send()
        x_copy(j).wait_send()
    for k in range(2):
        c_copy(k).wait_send()
    for d in range(1, 4):
        ra_copy(d).wait_send()
        u_copy(d).wait_send()
    for cp in outs:
        cp.wait()


def body(
    queries, fresh_keys, fresh_values, paged_keys, paged_values, request_page_table,
    live_token_count, request_adapter_slot, adapters_in_use, adapter_pool_row,
    adapter_down_factors, adapter_up_factors, output_weight, gating,
):
    rows, width = queries.shape
    n_out = output_weight.shape[1]
    half = n_out // 2
    hbm = pl.BlockSpec(memory_space=pl.ANY)
    smem = pl.BlockSpec(memory_space=pltpu.SMEM)
    V = pltpu.VMEM
    dma = pltpu.SemaphoreType.DMA
    pair = (2, 2 * RANK, width)
    return pl.pallas_call(
        kernel,
        out_shape=jax.ShapeDtypeStruct((rows // 4, n_out), BF),
        in_specs=[hbm] * 9 + [smem] * 5,
        out_specs=hbm,
        scratch_shapes=[
            V((rows, width), BF), V((rows, width), BF), V((rows, width), BF),
            V(paged_keys.shape, BF), V(paged_values.shape, BF), V((width, n_out), BF), V(gating.shape, F32),
            V((8, 128, width), BF),
            V((4, 128, half), BF), V((4, 128, half), BF), V((4, 128, half), F32), V((4, 128, half), BF),
            V((2, 128, n_out), BF), V((2, 128, n_out), BF), V((2, 128, n_out), F32),
            V((2, 2, 128, half), BF), V((2, 128, n_out), BF),
            V((Z, 2 * RANK, width), BF), V((Y, *pair), BF), V((2, *pair), BF), V((Z, *pair), BF),
            V((4, 2, RANK, 128), F32), V((4, 2, RANK, width), BF),
            V((4, 2, RANK, 128), F32), V((4, 2, RANK, width), BF),
            dma((12,)), dma((2, 2)),
            dma((4,)), dma((4,)), dma((4,)), dma((2, 2)), dma((2,)), dma((2,)),
            dma((Z,)), dma((Z,)), dma((Y,)), dma((Y,)), dma((1,)), dma((1,)), dma((Z,)), dma((Z,)),
            dma((4,)), dma((4,)), dma((4,)), dma((4,)),
        ],
        compiler_params=pltpu.CompilerParams(
            collective_id=0, has_side_effects=True, vmem_limit_bytes=60 * 1024 * 1024
        ),
        name="attend_project",
    )(
        queries, fresh_keys, fresh_values, paged_keys, paged_values,
        adapter_down_factors, adapter_up_factors, output_weight, gating,
        request_page_table, live_token_count, request_adapter_slot, adapters_in_use, adapter_pool_row,
    )


def solution(mesh):
    return jax.shard_map(
        body,
        mesh=mesh,
        in_specs=(
            P("req", "tp"), P("req", "tp"), P("req", "tp"),
            P("req", None, "tp"), P("req", None, "tp"),
            P("req", None), P("req"), P("req"), P(), P(),
            P("req", None, "tp"), P("req", None, None), P("tp", None), P("req", None),
        ),
        out_specs=P(("req", "tp"), None),
        check_vma=False,
    )
```

time: 381 us -> 61.3 us (0.16)
  local copies, waits for them, and re-layouts: 133 us -> 2.46 us
  waiting for transfers between devices: 108 us -> 0 us
  matrix products: 61.6 us -> 0 us
  Pallas kernels: 0 us -> 58.5 us
  starting transfers between devices: 44.9 us -> 0 us
  other arithmetic: 16.1 us -> 0 us
  between operations: 14.9 us -> 0.01 us
    all_gather x1 -> x0, waiting for transfers between devices: 102 us -> none  [sent_together(): result, at, done = (lax.all_gather(both, axis, axis=dim, tiled=True), 0, [])]
    concatenate x8 -> x0, local copies, waits for them, and re-layouts: 95.5 us -> none  [the longest x4 52.4 us: attend(): jnp.concatenate([cached_values, fresh_values.reshape(requests_here, slot_...]
    dot_general x8 -> x0, matrix products: 61.6 us -> none  [the longest x1 16.4 us: attend(): jnp.einsum('rhqk,rkhd->rqhd', rounded, values_all, preferred_element_type...]
    pallas_call x0 -> x1, Pallas kernels: none -> 58.5 us  [body(): pl.pallas_call(kernel, out_shape=jax.ShapeDtypeStruct((rows // 4, n_out),...]
    all_to_all x1 -> x0, starting transfers between devices: 44.8 us -> none  [from_everyone(): return lax.all_to_all(copies, axis, split_axis=0, concat_axis=0, tiled=True)]
    gather x3 -> x0, local copies, waits for them, and re-layouts: 17.6 us -> none  [the longest x1 8.46 us: attend(): paged_keys[request_page_table].reshape(requests_here, -1, feature_width)]
    reduce_sum x2 -> x0, other arithmetic: 13.5 us -> none  [the longest x1 11 us: attend(): row_total = jnp.sum(weights, axis=-1)]
    slice x2 -> x0, local copies, waits for them, and re-layouts: 7.67 us -> none  [sent_together(): done.append(lax.slice_in_dim(result, at, at + a.shape[along], axis=along))]
  transfers between devices with their start and end apart: 3 -> 0, of which waited for: 2 -> 0; matrix products, arithmetic and copies ran while one was open for 53% -> 0% of each run, Pallas kernels for 0% -> 0%
where the time goes in v1:
time: 61.3 us; the launch traced here: 61 us
  Pallas kernels  58.5 us (95%)
  local copies, waits for them, and re-layouts  2.46 us (4%)
    pallas_call x1, Pallas kernels, body(): pl.pallas_call(kernel, out_shape=jax.ShapeDtypeStruct((rows // 4, n_out),...  58.5 us
    unnamed x1, local copies, waits for them, and re-layouts  2.46 us

profile of v1, /device:TPU:1, one launch (start us, length us, event | category | flops | bytes accessed | tf_op | source)
XLA Modules:
  0.0 61.0 jit_solution(17025594803876060317)
XLA Ops:
  0.0 58.5 %attend_project.1 = bf16[256,2560]{1,0:T(8,128)(2,1)} custom-call(bf16[1024,640]{1,0:T(8,128)(2,1)} %q_hbm.1, bf16[1024,640]{1,0:T(8,128)(2,1)} %fk_hbm.1, bf16[1024,640]{1,0:T(8,128)(2,1)} %fv_hbm.1, bf16[16,128,640]{2,1,0:T(8,128)(2,1)} %kp_hbm.1, bf16[16,128,640]{2,1,0:T(8,128)(2,1)} %vp_hbm.1, bf16[1,16,640]{2,1,0:T(8,128)(2,1)} %down_hbm.1, ...), custom_call_target="tpu_custom_call" | custom-call | tf_op jit(solution)/shard_map/attend_project/pallas_call | solution.py:331
  58.5 2.5 %copy.16 = bf16[256,2560]{1,0:T(8,128)(2,1)} copy(bf16[256,2560]{1,0:T(8,128)(2,1)} %attend_project.1) | data formatting | bytes 2621440

commit v2 on v1

v2 whole, which is shorter than its diff:
```python
import functools
import math

import jax
import jax.numpy as jnp
from jax import lax
from jax.experimental import pallas as pl
from jax.experimental.pallas import tpu as pltpu
from jax.sharding import PartitionSpec as P

HD = 128
RANK = 16
MESH = pl.DeviceIdType.MESH
NEG = -1e30
SCALE = math.log2(math.e) / math.sqrt(HD)
BF = jnp.bfloat16
F32 = jnp.float32
Y, XLO, Z = 4, 2, 8
EVENTS = {
    (1, "b"): "sum", (4, "b"): "spread",
    (6, "a"): "f17", (6, "b"): "f26", (7, "a"): "f35", (7, "b"): "f4",
}


def kernel(
    q_hbm, fk_hbm, fv_hbm, kp_hbm, vp_hbm, down_hbm, up_hbm, w_hbm,
    pt, live, slot_of, in_use, pool_row,
    out,
    q, fk, fv, kp, vp, w,
    sbuf, pbuf, att, psend, precv, pkeep, xsend, csend, crecv, acc, xrecv,
    yrow, rs_send, rs_recv, gbuf, rbuf, ubuf, rsend, usend,
    lsem,
    p_s, p_r, x_s, x_r, c_s, c_r, y_s, y_r, z_s, z_r, g_s, g_r, f_s, f_r, ra_s, ra_r, u_s, u_r,
):
    req = lax.axis_index("req")
    tp = lax.axis_index("tp")
    z = lax.rem(req, Z)
    yx = req // Z
    y = yx // XLO
    xlo = lax.rem(yx, XLO)
    hi = tp // 2
    core = lax.rem(tp, 2)
    width = q.shape[1]
    heads = width // HD
    n_out = w.shape[1]
    half = n_out // 2

    def at(y_, xlo_, z_):
        return (y_ * XLO + xlo_) * Z + z_

    partner = (req, hi * 2 + 1 - core)
    tp_peer = lambda d: (req, lax.rem(tp + d, 4))
    z_peer = lambda d: (at(y, xlo, lax.rem(z + d, Z)), tp)
    y_peer = lambda d: (at(lax.rem(y + d, Y), xlo, z), tp)

    def plane_peer(e):
        return (at(lax.rem(y + e // 2, Y), lax.rem(xlo + e, 2), z), tp)


    first = pl.multiple_of((1 - hi) * 512, 512)
    second = pl.multiple_of(hi * 512, 512)
    loads = []

    def load(src, dst):
        cp = pltpu.make_async_copy(src, dst, lsem.at[len(loads)])
        cp.start()
        loads.append(cp)
        return cp

    own_down = load(down_hbm.at[0], yrow.at[0, pl.ds(0, RANK)])
    own_up = load(
        up_hbm.at[0, :, pl.ds(pl.multiple_of(tp * width, width), width)],
        yrow.at[0, pl.ds(RANK, RANK)],
    )
    early = [
        load(kp_hbm, kp),
        load(q_hbm.at[pl.ds(first, 512)], q.at[pl.ds(first, 512)]),
        load(fk_hbm.at[pl.ds(first, 512)], fk.at[pl.ds(first, 512)]),
        load(vp_hbm, vp),
        load(fv_hbm.at[pl.ds(first, 512)], fv.at[pl.ds(first, 512)]),
    ]
    load_w = load(w_hbm, w)
    late = [
        load(q_hbm.at[pl.ds(second, 512)], q.at[pl.ds(second, 512)]),
        load(fk_hbm.at[pl.ds(second, 512)], fk.at[pl.ds(second, 512)]),
        load(fv_hbm.at[pl.ds(second, 512)], fv.at[pl.ds(second, 512)]),
    ]

    barrier = pltpu.get_barrier_semaphore()
    peers = [tp_peer(d) for d in range(1, 4)] + [z_peer(d) for d in range(1, Z)]
    peers += [plane_peer(e) for e in range(1, Y * XLO)]
    for p in peers:
        pl.semaphore_signal(barrier, inc=1, device_id=p, device_id_type=MESH)
    pl.semaphore_wait(barrier, len(peers))

    def remote(src, dst, ss, rs, dev):
        return pltpu.make_async_remote_copy(src, dst, ss, rs, device_id=dev, device_id_type=MESH)

    def all_recv(buf, rs):
        remote(buf, buf, z_s.at[0], rs, partner).wait_recv()

    def all_sent(buf, ss):
        remote(buf, buf, ss, z_r.at[0], partner).wait_send()

    own_down.wait()
    own_up.wait()
    for e in range(1, Y * XLO):
        remote(yrow.at[0], yrow.at[e], y_s.at[0], y_r.at[0], plane_peer(e)).start()

    def phase_sum():
        all_recv(yrow.at[pl.ds(1, Y * XLO - 1)], y_r.at[0])
        for d in range(Z):
            p = lax.rem(z + d, Z)
            holder = pool_row[in_use[4 * y + p // 2]]
            part = pl.multiple_of(lax.rem(p, 2) * RANK, RANK)
            line = holder // Z
            place = lax.rem(y - line // XLO + Y, Y) * XLO + lax.rem(xlo + line, XLO)
            row = yrow[place, pl.ds(part, RANK)].astype(F32)
            piece = jnp.where(lax.rem(holder, Z) == z, row, 0.0).astype(BF)
            if d == 0:
                rs_recv[0] = piece
            else:
                rs_send[d - 1] = piece
                remote(rs_send.at[d - 1], rs_recv.at[d], z_s.at[0], z_r.at[0], z_peer(d)).start()

    def g_copy(d):
        return remote(gbuf.at[0, 0], gbuf.at[0, d], g_s.at[0], g_r.at[d], z_peer(d))

    def forward(d):
        for e in range(1, Y):
            remote(gbuf.at[0, d], gbuf.at[e, d], f_s.at[0], f_r.at[0], y_peer(e)).start()

    def phase_spread():
        all_recv(rs_recv.at[pl.ds(1, Z - 1)], z_r.at[0])
        total = rs_recv[0].astype(F32)
        for d in range(1, Z):
            total = total + rs_recv[d].astype(F32)
        gbuf[0, 0] = total.astype(BF)
        for d in (4, 3, 5, 2, 6, 1, 7):
            g_copy(d).start()
        forward(0)

    def phase_forward(*ds):
        for d in ds:
            g_copy(d).wait_recv()
            forward(d)

    p_copy = lambda j: remote(psend.at[j], precv.at[j], p_s.at[0], p_r.at[j], partner)
    c_copy = lambda k: remote(csend.at[k], crecv.at[k], c_s.at[0], c_r.at[0], partner)

    def x_copy(j):
        return remote(
            xsend.at[j], xrecv.at[lax.rem(j, 2), core],
            x_s.at[0], x_r.at[lax.rem(j, 2), core],
            (req, (1 - hi) * 2 + j // 2),
        )

    def project(a, base, chunk):
        return jnp.dot(
            a, w[:, pl.ds(pl.multiple_of(base, 128), chunk)], preferred_element_type=F32
        )

    mine = pl.multiple_of(core * half, half)
    other = pl.multiple_of((1 - core) * half, half)
    CH = 1280

    def pickup(j):
        p_copy(j).wait_recv()
        for n in range(0, half, CH):
            cols = pl.ds(n, CH)
            xsend[j, :, cols] = (pkeep[j, :, cols] + precv[j, :, cols].astype(F32)).astype(BF)
        x_copy(j).start()

    def request_of(step):
        there = (1 - hi) * 4 + step
        partners = hi * 4 + (1 - core) * 2 + step - 4
        own = hi * 4 + core * 2 + step - 6
        return jnp.where(step < 4, there, jnp.where(step < 6, partners, own))

    contract = (((1,), (1,)), ((), ()))

    def score(r, h, pages, count):
        cols = pl.ds(h * HD, HD)
        rows = pl.ds(pl.multiple_of(r * 128, 128), 128)
        qh = q[rows, cols]
        for g in range(0, 8, 2):
            k2 = jnp.concatenate([kp[pages[g], :, cols], kp[pages[g + 1], :, cols]], axis=0)
            s = lax.dot_general(qh, k2, contract, preferred_element_type=F32)
            sbuf[h % 2, :, pl.ds(g * 128, 256)] = s
        fresh = lax.dot_general(qh, fk[rows, cols], contract, preferred_element_type=F32)
        key_at = lax.broadcasted_iota(jnp.int32, fresh.shape, 1)
        sbuf[h % 2, :, pl.ds(1024, 128)] = jnp.where(key_at < count, fresh, NEG)

    def weigh(h):
        s = sbuf[h % 2]
        peak = jnp.max(s, axis=1, keepdims=True)
        p = jnp.exp2((s - peak) * SCALE)
        pbuf[h % 2] = p.astype(BF)
        return jnp.sum(p, axis=1, keepdims=True)

    def blend(r, h, pages, count, total):
        cols = pl.ds(h * HD, HD)
        rows = pl.ds(pl.multiple_of(r * 128, 128), 128)
        v = jnp.concatenate([vp[pages[g], :, cols] for g in range(8)] + [fv[rows, cols]], axis=0)
        o = jnp.dot(pbuf[h % 2], v, preferred_element_type=F32) / total
        slot_at = lax.broadcasted_iota(jnp.int32, o.shape, 0)
        att[r, :, cols] = jnp.where(slot_at < count, o, 0.0).astype(BF)

    for cp in early:
        cp.wait()

    events = EVENTS

    def step_body(step, carry):
        r = request_of(step)
        pages = [pt[r, g] for g in range(8)]
        count = live[r]

        def at_step(n, fn):
            pl.when(step == n)(fn)

        def run_events(gap):
            for (n, g), name in events.items():
                if g == gap:
                    at_step(n, phases[name])

        def wait_late():
            for cp in late:
                cp.wait()

        at_step(4, wait_late)

        totals = {}
        score(r, 0, pages, count)
        for h in range(heads + 1):
            if h + 1 < heads:
                score(r, h + 1, pages, count)
            if h >= 1:
                blend(r, h - 1, pages, count, totals[h - 1])
            if h < heads:
                totals[h] = weigh(h)

        pl.when((step >= 1) & (step <= 4))(lambda: pickup(step - 1))
        run_events("a")
        at_step(0, load_w.wait)
        a = att[r]

        @pl.when(step < 4)
        def _():
            psend[step] = project(a, other, half).astype(BF)
            p_copy(step).start()
            pkeep[step] = project(a, mine, half)

        @pl.when((step >= 4) & (step < 6))
        def _():
            for n in range(0, n_out, CH):
                csend[step - 4, :, pl.ds(n, CH)] = project(a, n, CH).astype(BF)
            c_copy(step - 4).start()

        @pl.when(step >= 6)
        def _():
            for n in range(0, n_out, CH):
                acc[step - 6, :, pl.ds(n, CH)] = project(a, n, CH)

        run_events("b")
        return carry

    phases = {
        "sum": phase_sum,
        "spread": phase_spread,
        "f17": lambda: phase_forward(1, 7),
        "f26": lambda: phase_forward(2, 6),
        "f35": lambda: phase_forward(3, 5),
        "f4": lambda: phase_forward(4),
    }
    lax.fori_loop(0, 8, step_body, 0)

    all_recv(gbuf.at[pl.ds(1, Y - 1)], f_r.at[0])
    ra_copy = lambda d: remote(rsend.at[d - 1], rbuf.at[d], ra_s.at[0], ra_r.at[0], tp_peer(d))
    u_copy = lambda d: remote(usend.at[d - 1], ubuf.at[d], u_s.at[0], u_r.at[0], tp_peer(d))
    for d in (2, 3, 1, 0):
        for k in range(2):
            r = lax.rem(tp + d, 4) * 2 + k
            s = slot_of[r]
            group = lax.rem(y - s // 4 + Y, Y)
            p = lax.rem(s, 4) * 2
            down = gbuf[group, lax.rem(z - p + Z, Z)]
            up = gbuf[group, lax.rem(z - p - 1 + Z, Z)]
            ranked = lax.dot_general(
                down, att[r], (((1,), (1,)), ((), ())), preferred_element_type=F32
            )
            if d == 0:
                rbuf[0, k] = ranked
                ubuf[0, k] = up
            else:
                rsend[d - 1, k] = ranked
                usend[d - 1, k] = up
        if d:
            ra_copy(d).start()
            u_copy(d).start()

    all_recv(crecv, c_r.at[0])
    all_recv(rbuf.at[pl.ds(1, 3)], ra_r.at[0])
    all_recv(ubuf.at[pl.ds(1, 3)], u_r.at[0])

    for k in range(2):
        ra = rbuf[0, k] + rbuf[1, k] + rbuf[2, k] + rbuf[3, k]
        top = ra.astype(BF)
        rest = ra - top.astype(F32)
        mid = rest.astype(BF)
        low = (rest - mid.astype(F32)).astype(BF)
        ra3 = jnp.concatenate([top, mid, low], axis=0)
        for n in range(4):
            cols = pl.ds(n * width, width)
            u1 = ubuf[lax.rem(tp - n + 4, 4), k]
            u3 = jnp.concatenate([u1, u1, u1], axis=0)
            term = lax.dot_general(ra3, u3, (((0,), (0,)), ((), ())), preferred_element_type=F32)
            acc[k, :, cols] = acc[k, :, cols] + crecv[k, :, cols].astype(F32) + term

    for k in range(2):
        for cs in range(2):
            remote(xsend.at[0], xrecv.at[k, cs], x_s.at[0], x_r.at[k, cs], partner).wait_recv()
            cols = pl.ds(cs * half, half)
            out[pl.ds(k * 128, 128), cols] = acc[k, :, cols] + xrecv[k, cs].astype(F32)

    all_sent(yrow.at[pl.ds(1, Y * XLO - 1)], y_s.at[0])
    all_sent(rs_send, z_s.at[0])
    all_sent(gbuf.at[0, pl.ds(1, Z - 1)], g_s.at[0])
    all_sent(gbuf.at[pl.ds(1, Y - 1)], f_s.at[0])
    all_sent(psend, p_s.at[0])
    all_sent(xsend, x_s.at[0])
    all_sent(csend, c_s.at[0])
    all_sent(rsend, ra_s.at[0])
    all_sent(usend, u_s.at[0])


def body(
    queries, fresh_keys, fresh_values, paged_keys, paged_values, request_page_table,
    live_token_count, request_adapter_slot, adapters_in_use, adapter_pool_row,
    adapter_down_factors, adapter_up_factors, output_weight, gating,
):
    rows, width = queries.shape
    n_out = output_weight.shape[1]
    half = n_out // 2
    hbm = pl.BlockSpec(memory_space=pltpu.HBM)
    smem = pl.BlockSpec(memory_space=pltpu.SMEM)
    V = pltpu.VMEM
    dma = pltpu.SemaphoreType.DMA
    one = dma((1,))
    def pinned(*xs):
        return [pltpu.with_memory_space_constraint(x, pltpu.HBM) for x in xs]

    total = pl.pallas_call(
        kernel,
        out_shape=jax.ShapeDtypeStruct((rows // 4, n_out), F32),
        in_specs=[hbm] * 8 + [smem] * 5,
        out_specs=pl.BlockSpec(memory_space=V),
        scratch_shapes=[
            V((rows, width), BF), V((rows, width), BF), V((rows, width), BF),
            V(paged_keys.shape, BF), V(paged_values.shape, BF), V((width, n_out), BF),
            V((2, 128, 1152), F32), V((2, 128, 1152), BF), V((8, 128, width), BF),
            V((4, 128, half), BF), V((4, 128, half), BF), V((4, 128, half), F32), V((4, 128, half), BF),
            V((2, 128, n_out), BF), V((2, 128, n_out), BF), V((2, 128, n_out), F32),
            V((2, 2, 128, half), BF),
            V((Y * XLO, 2 * RANK, width), BF), V((Z - 1, RANK, width), BF), V((Z, RANK, width), BF),
            V((Y, Z, RANK, width), BF),
            V((4, 2, RANK, 128), F32), V((4, 2, RANK, width), BF),
            V((3, 2, RANK, 128), F32), V((3, 2, RANK, width), BF),
            dma((11,)),
            one, dma((4,)), one, dma((2, 2)), one, one, one, one, one, one,
            one, dma((Z,)), one, one, one, one, one, one,
        ],
        compiler_params=pltpu.CompilerParams(
            collective_id=0, has_side_effects=True, vmem_limit_bytes=48 * 1024 * 1024
        ),
        name="attend_project",
    )(
        *pinned(
            queries, fresh_keys, fresh_values, paged_keys, paged_values,
            adapter_down_factors, adapter_up_factors, output_weight,
            request_page_table, live_token_count, request_adapter_slot, adapters_in_use, adapter_pool_row,
        )
    )
    gate = lax.dynamic_slice_in_dim(gating, lax.axis_index("tp") * 2, 2, 0)
    gated = gate[:, None, :] * total.reshape(2, -1, n_out)
    return gated.reshape(-1, n_out).astype(BF)


def solution(mesh):
    return jax.shard_map(
        body,
        mesh=mesh,
        in_specs=(
            P("req", "tp"), P("req", "tp"), P("req", "tp"),
            P("req", None, "tp"), P("req", None, "tp"),
            P("req", None), P("req"), P("req"), P(), P(),
            P("req", None, "tp"), P("req", None, None), P("tp", None), P("req", None),
        ),
        out_specs=P(("req", "tp"), None),
        check_vma=False,
    )
```

time: 61.3 us -> 50.5 us (0.82)
  Pallas kernels: 58.5 us -> 48.3 us
  local copies, waits for them, and re-layouts: 2.46 us -> 0.9 us
  other arithmetic: 0 us -> 1.22 us
    pallas_call x1, Pallas kernels: 58.5 us -> 48.3 us  [body(): pl.pallas_call(kernel, out_shape=jax.ShapeDtypeStruct((rows // 4, n_out),...]
    unnamed x1 -> x2, local copies, waits for them, and re-layouts: 2.46 us -> 0.89 us
    convert_element_type x0 -> x1, other arithmetic: none -> 1.22 us  [body(): return gated.reshape(-1, n_out).astype(BF)]
where the time goes in v2:
time: 50.5 us; the launch traced here: 50.4 us
  Pallas kernels  48.3 us (96%)
  other arithmetic  1.22 us (2%)
  local copies, waits for them, and re-layouts  0.9 us (2%)
    pallas_call x1, Pallas kernels, body(): pl.pallas_call(kernel, out_shape=jax.ShapeDtypeStruct((rows // 4, n_out),...  48.3 us
    convert_element_type x1, other arithmetic, body(): return gated.reshape(-1, n_out).astype(BF)  1.22 us

profile of v2, /device:TPU:1, one launch (start us, length us, event | category | flops | bytes accessed | tf_op | source)
XLA Modules:
  0.0 50.4 jit_solution(5902895692884104783)
XLA Ops:
  0.0 0.0 copy-start
  0.0 0.9 %copy-done = f32[8,2560]{1,0:T(8,128)S(1)} copy-done((f32[8,2560]{1,0:T(8,128)S(1)}, f32[8,2560]{1,0:T(8,128)}, u32[]{:S(2)}) %copy-start) | copy-done | bytes 81944
  0.9 48.3 %attend_project.1 = f32[256,2560]{1,0:T(8,128)S(1)} custom-call(bf16[1024,640]{1,0:T(8,128)(2,1)} %q_hbm.1, bf16[1024,640]{1,0:T(8,128)(2,1)} %fk_hbm.1, bf16[1024,640]{1,0:T(8,128)(2,1)} %fv_hbm.1, bf16[16,128,640]{2,1,0:T(8,128)(2,1)} %kp_hbm.1, bf16[16,128,640]{2,1,0:T(8,128)(2,1)} %vp_hbm.1, bf16[1,16,640]{2,1,0:T(8,128)(2,1)} %down_hbm.1, ...), custom_call_target="tpu_custom_call" | custom-call | tf_op jit(solution)/shard_map/attend_project/pallas_call | solution.py:353
  49.2 1.2 %fusion = bf16[256,2560]{1,0:T(8,128)(2,1)} fusion(f32[256,2560]{1,0:T(8,128)S(1)} %attend_project.1, f32[2,2560]{1,0:T(2,128)S(1)} %constant_dynamic-slice_fusion), kind=kLoop, calls=%fused_computation.1 | loop fusion | flops 1310720 | bytes 3952640 | tf_op jit(solution)/shard_map/convert_element_type | solution.py:386
  (1 shorter events, 0.0 us)
Async XLA Ops:
  0.0 0.9 %copy-start = (f32[8,2560]{1,0:T(8,128)S(1)}, f32[8,2560]{1,0:T(8,128)}, u32[]{:S(2)}) copy-start(f32[8,2560]{1,0:T(8,128)} %param.27) | copy-start | bytes 245764

commit v3 on v2

--- a/solution.py
+++ b/solution.py
@@ -17,8 +17,8 @@
 F32 = jnp.float32
 Y, XLO, Z = 4, 2, 8
 EVENTS = {
-    (1, "b"): "sum", (4, "b"): "spread",
-    (6, "a"): "f17", (6, "b"): "f26", (7, "a"): "f35", (7, "b"): "f4",
+    (1, "a"): "sum", (3, "b"): "spread",
+    (5, "a"): "f17", (5, "b"): "f26", (6, "a"): "f35", (6, "b"): "f4",
 }
 
 
@@ -72,14 +72,20 @@
         up_hbm.at[0, :, pl.ds(pl.multiple_of(tp * width, width), width)],
         yrow.at[0, pl.ds(RANK, RANK)],
     )
+    rest = pl.multiple_of(first + 128, 128)
     early = [
         load(kp_hbm, kp),
-        load(q_hbm.at[pl.ds(first, 512)], q.at[pl.ds(first, 512)]),
-        load(fk_hbm.at[pl.ds(first, 512)], fk.at[pl.ds(first, 512)]),
+        load(q_hbm.at[pl.ds(first, 128)], q.at[pl.ds(first, 128)]),
+        load(fk_hbm.at[pl.ds(first, 128)], fk.at[pl.ds(first, 128)]),
         load(vp_hbm, vp),
-        load(fv_hbm.at[pl.ds(first, 512)], fv.at[pl.ds(first, 512)]),
+        load(fv_hbm.at[pl.ds(first, 128)], fv.at[pl.ds(first, 128)]),
     ]
     load_w = load(w_hbm, w)
+    following = [
+        load(q_hbm.at[pl.ds(rest, 384)], q.at[pl.ds(rest, 384)]),
+        load(fk_hbm.at[pl.ds(rest, 384)], fk.at[pl.ds(rest, 384)]),
+        load(fv_hbm.at[pl.ds(rest, 384)], fv.at[pl.ds(rest, 384)]),
+    ]
     late = [
         load(q_hbm.at[pl.ds(second, 512)], q.at[pl.ds(second, 512)]),
         load(fk_hbm.at[pl.ds(second, 512)], fk.at[pl.ds(second, 512)]),
@@ -145,12 +151,20 @@
             g_copy(d).wait_recv()
             forward(d)
 
-    p_copy = lambda j: remote(psend.at[j], precv.at[j], p_s.at[0], p_r.at[j], partner)
+    HALF = half // 2
+
+    def p_copy(j, c):
+        cols = pl.ds(c * HALF, HALF)
+        return remote(
+            psend.at[j, :, cols], precv.at[j, :, cols], p_s.at[0], p_r.at[j, c], partner
+        )
+
     c_copy = lambda k: remote(csend.at[k], crecv.at[k], c_s.at[0], c_r.at[0], partner)
 
-    def x_copy(j):
+    def x_copy(j, c):
+        cols = pl.ds(c * HALF, HALF)
         return remote(
-            xsend.at[j], xrecv.at[lax.rem(j, 2), core],
+            xsend.at[j, :, cols], xrecv.at[lax.rem(j, 2), core, :, cols],
             x_s.at[0], x_r.at[lax.rem(j, 2), core],
             (req, (1 - hi) * 2 + j // 2),
         )
@@ -165,11 +179,14 @@
     CH = 1280
 
     def pickup(j):
-        p_copy(j).wait_recv()
-        for n in range(0, half, CH):
-            cols = pl.ds(n, CH)
+        for c in range(2):
+            p_copy(j, c).wait_recv()
+            cols = pl.ds(c * HALF, HALF)
             xsend[j, :, cols] = (pkeep[j, :, cols] + precv[j, :, cols].astype(F32)).astype(BF)
-        x_copy(j).start()
+            if c == 0:
+                x_copy(j, 0).start()
+            else:
+                pl.when(j < 3)(lambda: x_copy(j, 1).start())
 
     def request_of(step):
         there = (1 - hi) * 4 + step
@@ -228,6 +245,11 @@
             for cp in late:
                 cp.wait()
 
+        def wait_following():
+            for cp in following:
+                cp.wait()
+
+        at_step(1, wait_following)
         at_step(4, wait_late)
 
         totals = {}
@@ -240,15 +262,16 @@
             if h < heads:
                 totals[h] = weigh(h)
 
-        pl.when((step >= 1) & (step <= 4))(lambda: pickup(step - 1))
+        pl.when((step >= 2) & (step <= 4))(lambda: pickup(step - 1))
         run_events("a")
         at_step(0, load_w.wait)
         a = att[r]
 
         @pl.when(step < 4)
         def _():
-            psend[step] = project(a, other, half).astype(BF)
-            p_copy(step).start()
+            for c in range(2):
+                psend[step, :, pl.ds(c * HALF, HALF)] = project(a, other + c * HALF, HALF).astype(BF)
+                p_copy(step, c).start()
             pkeep[step] = project(a, mine, half)
 
         @pl.when((step >= 4) & (step < 6))
@@ -262,6 +285,7 @@
             for n in range(0, n_out, CH):
                 acc[step - 6, :, pl.ds(n, CH)] = project(a, n, CH)
 
+        at_step(0, lambda: pickup(0))
         run_events("b")
         return carry
 
@@ -299,6 +323,7 @@
             ra_copy(d).start()
             u_copy(d).start()
 
+    x_copy(3, 1).start()
     all_recv(crecv, c_r.at[0])
     all_recv(rbuf.at[pl.ds(1, 3)], ra_r.at[0])
     all_recv(ubuf.at[pl.ds(1, 3)], u_r.at[0])
@@ -366,8 +391,8 @@
             V((Y, Z, RANK, width), BF),
             V((4, 2, RANK, 128), F32), V((4, 2, RANK, width), BF),
             V((3, 2, RANK, 128), F32), V((3, 2, RANK, width), BF),
-            dma((11,)),
-            one, dma((4,)), one, dma((2, 2)), one, one, one, one, one, one,
+            dma((14,)),
+            one, dma((4, 2)), one, dma((2, 2)), one, one, one, one, one, one,
             one, dma((Z,)), one, one, one, one, one, one,
         ],
         compiler_params=pltpu.CompilerParams(

time: 50.5 us -> 49.6 us (0.982)
  Pallas kernels: 48.3 us -> 47.3 us
    pallas_call x1, Pallas kernels: 48.3 us -> 47.3 us  [body(): pl.pallas_call(kernel, out_shape=jax.ShapeDtypeStruct((rows // 4, n_out),...]
where the time goes in v3:
time: 49.6 us; the launch traced here: 49.5 us
  Pallas kernels  47.3 us (95%)
  other arithmetic  1.22 us (2%)
  local copies, waits for them, and re-layouts  0.9 us (2%)
    pallas_call x1, Pallas kernels, body(): pl.pallas_call(kernel, out_shape=jax.ShapeDtypeStruct((rows // 4, n_out),...  47.3 us
    convert_element_type x1, other arithmetic, body(): return gated.reshape(-1, n_out).astype(BF)  1.22 us

profile of v3, /device:TPU:1, one launch (start us, length us, event | category | flops | bytes accessed | tf_op | source)
XLA Modules:
  0.0 49.5 jit_solution(1725795236195564445)
XLA Ops:
  0.0 0.0 copy-start
  0.0 0.9 %copy-done = f32[8,2560]{1,0:T(8,128)S(1)} copy-done((f32[8,2560]{1,0:T(8,128)S(1)}, f32[8,2560]{1,0:T(8,128)}, u32[]{:S(2)}) %copy-start) | copy-done | bytes 81944
  0.9 47.3 %attend_project.1 = f32[256,2560]{1,0:T(8,128)S(1)} custom-call(bf16[1024,640]{1,0:T(8,128)(2,1)} %q_hbm.1, bf16[1024,640]{1,0:T(8,128)(2,1)} %fk_hbm.1, bf16[1024,640]{1,0:T(8,128)(2,1)} %fv_hbm.1, bf16[16,128,640]{2,1,0:T(8,128)(2,1)} %kp_hbm.1, bf16[16,128,640]{2,1,0:T(8,128)(2,1)} %vp_hbm.1, bf16[1,16,640]{2,1,0:T(8,128)(2,1)} %down_hbm.1, ...), custom_call_target="tpu_custom_call" | custom-call | tf_op jit(solution)/shard_map/attend_project/pallas_call | solution.py:378
  48.2 1.2 %fusion = bf16[256,2560]{1,0:T(8,128)(2,1)} fusion(f32[256,2560]{1,0:T(8,128)S(1)} %attend_project.1, f32[2,2560]{1,0:T(2,128)S(1)} %constant_dynamic-slice_fusion), kind=kLoop, calls=%fused_computation.1 | loop fusion | flops 1310720 | bytes 3952640 | tf_op jit(solution)/shard_map/convert_element_type | solution.py:411
  (1 shorter events, 0.0 us)
Async XLA Ops:
  0.0 0.9 %copy-start = (f32[8,2560]{1,0:T(8,128)S(1)}, f32[8,2560]{1,0:T(8,128)}, u32[]{:S(2)}) copy-start(f32[8,2560]{1,0:T(8,128)} %param.27) | copy-start | bytes 245764

commit v4 on v3

--- a/solution.py
+++ b/solution.py
@@ -97,7 +97,6 @@
     peers += [plane_peer(e) for e in range(1, Y * XLO)]
     for p in peers:
         pl.semaphore_signal(barrier, inc=1, device_id=p, device_id_type=MESH)
-    pl.semaphore_wait(barrier, len(peers))
 
     def remote(src, dst, ss, rs, dev):
         return pltpu.make_async_remote_copy(src, dst, ss, rs, device_id=dev, device_id_type=MESH)
@@ -107,11 +106,6 @@
 
     def all_sent(buf, ss):
         remote(buf, buf, ss, z_r.at[0], partner).wait_send()
-
-    own_down.wait()
-    own_up.wait()
-    for e in range(1, Y * XLO):
-        remote(yrow.at[0], yrow.at[e], y_s.at[0], y_r.at[0], plane_peer(e)).start()
 
     def phase_sum():
         all_recv(yrow.at[pl.ds(1, Y * XLO - 1)], y_r.at[0])
@@ -223,45 +217,60 @@
         slot_at = lax.broadcasted_iota(jnp.int32, o.shape, 0)
         att[r, :, cols] = jnp.where(slot_at < count, o, 0.0).astype(BF)
 
-    for cp in early:
-        cp.wait()
-
-    events = EVENTS
-
-    def step_body(step, carry):
-        r = request_of(step)
+    def attend(r, between=None):
         pages = [pt[r, g] for g in range(8)]
         count = live[r]
-
-        def at_step(n, fn):
-            pl.when(step == n)(fn)
-
-        def run_events(gap):
-            for (n, g), name in events.items():
-                if g == gap:
-                    at_step(n, phases[name])
-
-        def wait_late():
-            for cp in late:
-                cp.wait()
-
-        def wait_following():
-            for cp in following:
-                cp.wait()
-
-        at_step(1, wait_following)
-        at_step(4, wait_late)
-
         totals = {}
         score(r, 0, pages, count)
         for h in range(heads + 1):
             if h + 1 < heads:
                 score(r, h + 1, pages, count)
             if h >= 1:
+                if h == 1 and between:
+                    between()
                 blend(r, h - 1, pages, count, totals[h - 1])
             if h < heads:
                 totals[h] = weigh(h)
 
+    def wait_values():
+        for cp in early[3:]:
+            cp.wait()
+
+    for cp in early[:3]:
+        cp.wait()
+    attend((1 - hi) * 4, wait_values)
+
+    pl.semaphore_wait(barrier, len(peers))
+    own_down.wait()
+    own_up.wait()
+    for e in range(1, Y * XLO):
+        remote(yrow.at[0], yrow.at[e], y_s.at[0], y_r.at[0], plane_peer(e)).start()
+
+    events = EVENTS
+
+    def step_body(step, carry):
+        r = request_of(step)
+
+        def at_step(n, fn):
+            pl.when(step == n)(fn)
+
+        def run_events(gap):
+            for (n, g), name in events.items():
+                if g == gap:
+                    at_step(n, phases[name])
+
+        def wait_late():
+            for cp in late:
+                cp.wait()
+
+        def wait_following():
+            for cp in following:
+                cp.wait()
+
+        at_step(1, wait_following)
+        at_step(4, wait_late)
+
+        pl.when(step > 0)(lambda: attend(r))
         pl.when((step >= 2) & (step <= 4))(lambda: pickup(step - 1))
         run_events("a")
         at_step(0, load_w.wait)

time: 49.6 us -> 49.4 us (level)
  no operation moved by 1% of the time
where the time goes in v4:
time: 49.4 us; the launch traced here: 49.3 us
  Pallas kernels  47.1 us (95%)
  other arithmetic  1.22 us (2%)
  local copies, waits for them, and re-layouts  0.9 us (2%)
    pallas_call x1, Pallas kernels, body(): pl.pallas_call(kernel, out_shape=jax.ShapeDtypeStruct((rows // 4, n_out),...  47.1 us
    convert_element_type x1, other arithmetic, body(): return gated.reshape(-1, n_out).astype(BF)  1.22 us

profile of v4, /device:TPU:1, one launch (start us, length us, event | category | flops | bytes accessed | tf_op | source)
XLA Modules:
  0.0 49.3 jit_solution(12535803078399267419)
XLA Ops:
  0.0 0.0 copy-start
  0.0 0.9 %copy-done = f32[8,2560]{1,0:T(8,128)S(1)} copy-done((f32[8,2560]{1,0:T(8,128)S(1)}, f32[8,2560]{1,0:T(8,128)}, u32[]{:S(2)}) %copy-start) | copy-done | bytes 81944
  0.9 47.1 %attend_project.1 = f32[256,2560]{1,0:T(8,128)S(1)} custom-call(bf16[1024,640]{1,0:T(8,128)(2,1)} %q_hbm.1, bf16[1024,640]{1,0:T(8,128)(2,1)} %fk_hbm.1, bf16[1024,640]{1,0:T(8,128)(2,1)} %fv_hbm.1, bf16[16,128,640]{2,1,0:T(8,128)(2,1)} %kp_hbm.1, bf16[16,128,640]{2,1,0:T(8,128)(2,1)} %vp_hbm.1, bf16[1,16,640]{2,1,0:T(8,128)(2,1)} %down_hbm.1, ...), custom_call_target="tpu_custom_call" | custom-call | tf_op jit(solution)/shard_map/attend_project/pallas_call | solution.py:387
  48.1 1.2 %fusion = bf16[256,2560]{1,0:T(8,128)(2,1)} fusion(f32[256,2560]{1,0:T(8,128)S(1)} %attend_project.1, f32[2,2560]{1,0:T(2,128)S(1)} %constant_dynamic-slice_fusion), kind=kLoop, calls=%fused_computation.1 | loop fusion | flops 1310720 | bytes 3952640 | tf_op jit(solution)/shard_map/convert_element_type | solution.py:420
  (1 shorter events, 0.0 us)
Async XLA Ops:
  0.0 0.9 %copy-start = (f32[8,2560]{1,0:T(8,128)S(1)}, f32[8,2560]{1,0:T(8,128)}, u32[]{:S(2)}) copy-start(f32[8,2560]{1,0:T(8,128)} %param.27) | copy-start | bytes 245764

commit v5 on v4

--- a/solution.py
+++ b/solution.py
@@ -80,7 +80,10 @@
         load(vp_hbm, vp),
         load(fv_hbm.at[pl.ds(first, 128)], fv.at[pl.ds(first, 128)]),
     ]
-    load_w = load(w_hbm, w)
+    mine = pl.multiple_of(core * half, half)
+    other = pl.multiple_of((1 - core) * half, half)
+    load_w = load(w_hbm.at[:, pl.ds(other, half)], w.at[:, pl.ds(other, half)])
+    load_w_mine = load(w_hbm.at[:, pl.ds(mine, half)], w.at[:, pl.ds(mine, half)])
     following = [
         load(q_hbm.at[pl.ds(rest, 384)], q.at[pl.ds(rest, 384)]),
         load(fk_hbm.at[pl.ds(rest, 384)], fk.at[pl.ds(rest, 384)]),
@@ -168,8 +171,6 @@
             a, w[:, pl.ds(pl.multiple_of(base, 128), chunk)], preferred_element_type=F32
         )
 
-    mine = pl.multiple_of(core * half, half)
-    other = pl.multiple_of((1 - core) * half, half)
     CH = 1280
 
     def pickup(j):
@@ -281,6 +282,7 @@
             for c in range(2):
                 psend[step, :, pl.ds(c * HALF, HALF)] = project(a, other + c * HALF, HALF).astype(BF)
                 p_copy(step, c).start()
+            at_step(0, load_w_mine.wait)
             pkeep[step] = project(a, mine, half)
 
         @pl.when((step >= 4) & (step < 6))
@@ -400,7 +402,7 @@
             V((Y, Z, RANK, width), BF),
             V((4, 2, RANK, 128), F32), V((4, 2, RANK, width), BF),
             V((3, 2, RANK, 128), F32), V((3, 2, RANK, width), BF),
-            dma((14,)),
+            dma((15,)),
             one, dma((4, 2)), one, dma((2, 2)), one, one, one, one, one, one,
             one, dma((Z,)), one, one, one, one, one, one,
         ],

time: 49.4 us -> 49.4 us (level)
  no operation moved by 1% of the time
where the time goes in v5:
time: 49.4 us; the launch traced here: 49.3 us
  Pallas kernels  47.2 us (96%)
  other arithmetic  1.22 us (2%)
  local copies, waits for them, and re-layouts  0.9 us (2%)
    pallas_call x1, Pallas kernels, body(): pl.pallas_call(kernel, out_shape=jax.ShapeDtypeStruct((rows // 4, n_out),...  47.2 us
    convert_element_type x1, other arithmetic, body(): return gated.reshape(-1, n_out).astype(BF)  1.22 us

profile of v5, /device:TPU:1, one launch (start us, length us, event | category | flops | bytes accessed | tf_op | source)
XLA Modules:
  0.0 49.3 jit_solution(12156820079932390170)
XLA Ops:
  0.0 0.0 copy-start
  0.0 0.9 %copy-done = f32[8,2560]{1,0:T(8,128)S(1)} copy-done((f32[8,2560]{1,0:T(8,128)S(1)}, f32[8,2560]{1,0:T(8,128)}, u32[]{:S(2)}) %copy-start) | copy-done | bytes 81944
  0.9 47.2 %attend_project.1 = f32[256,2560]{1,0:T(8,128)S(1)} custom-call(bf16[1024,640]{1,0:T(8,128)(2,1)} %q_hbm.1, bf16[1024,640]{1,0:T(8,128)(2,1)} %fk_hbm.1, bf16[1024,640]{1,0:T(8,128)(2,1)} %fv_hbm.1, bf16[16,128,640]{2,1,0:T(8,128)(2,1)} %kp_hbm.1, bf16[16,128,640]{2,1,0:T(8,128)(2,1)} %vp_hbm.1, bf16[1,16,640]{2,1,0:T(8,128)(2,1)} %down_hbm.1, ...), custom_call_target="tpu_custom_call" | custom-call | tf_op jit(solution)/shard_map/attend_project/pallas_call | solution.py:389
  48.1 1.2 %fusion = bf16[256,2560]{1,0:T(8,128)(2,1)} fusion(f32[256,2560]{1,0:T(8,128)S(1)} %attend_project.1, f32[2,2560]{1,0:T(2,128)S(1)} %constant_dynamic-slice_fusion), kind=kLoop, calls=%fused_computation.1 | loop fusion | flops 1310720 | bytes 3952640 | tf_op jit(solution)/shard_map/convert_element_type | solution.py:422
  (1 shorter events, 0.0 us)
Async XLA Ops:
  0.0 0.9 %copy-start = (f32[8,2560]{1,0:T(8,128)S(1)}, f32[8,2560]{1,0:T(8,128)}, u32[]{:S(2)}) copy-start(f32[8,2560]{1,0:T(8,128)} %param.27) | copy-start | bytes 245764
